TPU v7x, 512 devices: a whole 4x4x16 slice. The times are simulated.
512 devices in a mesh: segment: 2 (over x_lo), seq: 32 (over z, core), tensor: 8 (over y, x_hi).
Axes of the slice: x: 4 (x_hi: 2, x_lo: 2; x = x_hi * 2 + x_lo), y: 4, z: 16, core: 2. Of those that a mesh axis runs over, the one named last changes fastest.
Arguments:
- vision_states: bfloat16 [6144, 7680], P(('segment', 'seq'), 'tensor'), may hold values from -6 to 6
- kv_weight: bfloat16 [7680, 2048], P('tensor'), may hold values from -0.09375 to 0.09375
- key_gain: float32 [128], replicated, may hold values from 0.5 to 1.5
- queries: bfloat16 [16384, 8, 1024], P('seq', 'tensor', 'segment'), may hold values from -700 to 700
- tile_tokens: int32 [4], replicated, may hold values from 768 to 1536, as said below
- text_tiles: int32 [16384, 2], P('seq'), may hold values from 0 to 4, as said below
Outputs:
- attended: bfloat16 [16384, 8, 1024], P('seq', 'tensor', 'segment')
Inputs may be any that keep to these rules, and one draw needn't show every extreme that they name: The valid tokens of tile i are its first tile_tokens[i] positions of 1536; some tile is full. Text token r sees tiles text_tiles[r, 0] to text_tiles[r, 1] - 1, with text_tiles[r, 0] <= text_tiles[r, 1]; an empty range means it sees no image.
All inputs are finite; a program needn't handle non-finite values.
Results may differ from a plain program's by a relative error of at most 0.012.
The roundings to bfloat16 on the way count: a program that leaves them out, or rounds other values in their place, can miss the bound.
Values may be sent and summed in bfloat16 or wider, within the bound.
A program may use at most 64 MiB of HBM per device.

v0:
```python
import jax
import jax.numpy as jnp
from jax import lax
from jax.sharding import PartitionSpec as P


def block_count(total_rows, limit_rows):
    for parts_count in range(1, total_rows + 1):
        if total_rows % parts_count == 0 and total_rows // parts_count <= limit_rows:
            return parts_count
    return total_rows


def visibility(positions, tile_len, tile_tokens, lower, upper):
    tile_ids = positions // tile_len
    within_tile = positions % tile_len
    tile_table = jnp.arange(tile_tokens.shape[0], dtype=jnp.int32)
    valid_count = jnp.sum(
        jnp.where(tile_ids[:, None] == tile_table[None, :], tile_tokens[None, :], 0), axis=-1
    )
    key_valid = within_tile < valid_count
    return (
        key_valid[None, :]
        & (tile_ids[None, :] >= lower[:, None])
        & (tile_ids[None, :] < upper[:, None])
    )


def update(running, query_heads, kv_piece, visible, score_scale, head_dim):
    row_max, row_sum, summed = running
    scores = (
        jnp.einsum(
            "rkhd,knd->rkhn",
            query_heads,
            kv_piece[:, :, :head_dim],
            preferred_element_type=jnp.float32,
        )
        * score_scale
    )
    key_mask = visible[:, None, None, :]
    masked = jnp.where(key_mask, scores, -1e30)
    new_max = jnp.maximum(row_max, jnp.max(masked, axis=-1))
    factor = jnp.exp(row_max - new_max)
    expterm = jnp.where(key_mask, jnp.exp(masked - new_max[..., None]), 0.0)
    row_sum = row_sum * factor + jnp.sum(expterm, axis=-1)
    weights = expterm.astype(jnp.bfloat16)
    summed = summed * factor[..., None] + jnp.einsum(
        "rkhn,knd->rkhd", weights, kv_piece[:, :, head_dim:], preferred_element_type=jnp.float32
    )
    return (new_max, row_sum, summed)


def shards(vision_states, kv_weight, key_gain, queries, tile_tokens, text_tiles):
    head_dim = key_gain.shape[0]
    key_rows = vision_states.shape[0]
    all_heads = kv_weight.shape[1] // (2 * head_dim)
    local_heads = all_heads // lax.axis_size("tensor")
    weight_heads = kv_weight.reshape(kv_weight.shape[0], all_heads, 2 * head_dim)
    sums = lax.psum_scatter(
        jnp.einsum("rd,dch->crh", vision_states, weight_heads, preferred_element_type=jnp.float32),
        "tensor",
        scatter_dimension=0,
        tiled=True,
    )
    keys_raw = sums[:, :, :head_dim]
    mean_sq = jnp.mean(keys_raw * keys_raw, axis=-1, keepdims=True)
    normed = keys_raw * lax.rsqrt(mean_sq + 1e-05) * key_gain
    kv_block = jnp.concatenate([normed, sums[:, :, head_dim:]], axis=-1).astype(jnp.bfloat16)
    segment_count = lax.axis_size("segment")
    seq_count = lax.axis_size("seq")
    tile_len = key_rows * segment_count * seq_count // tile_tokens.shape[0]
    text_rows = queries.shape[0]
    query_count = queries.shape[2] // head_dim
    query_heads = queries.reshape(text_rows, local_heads, query_count, head_dim)
    lower = text_tiles[:, 0]
    upper = text_tiles[:, 1]
    unseen = (upper <= lower).astype(jnp.float32)
    score_scale = head_dim ** (-0.5)
    start_state = (
        jnp.full((text_rows, local_heads, query_count), -1e30, jnp.float32),
        jnp.zeros((text_rows, local_heads, query_count), jnp.float32),
        jnp.zeros((text_rows, local_heads, query_count, head_dim), jnp.float32),
    )
    gathered = lax.all_gather(kv_block, ("segment", "seq"), axis=1, tiled=True)
    total_rows = gathered.shape[1]
    blocks = block_count(total_rows, 768)
    block_rows = total_rows // blocks

    def one_block(block_index, state_now):
        block_piece = lax.dynamic_slice_in_dim(gathered, block_index * block_rows, block_rows, 1)
        local_rows = block_index * block_rows + jnp.arange(block_rows, dtype=jnp.int32)
        visible = visibility(local_rows, tile_len, tile_tokens, lower, upper)
        return update(state_now, query_heads, block_piece, visible, score_scale, head_dim)

    row_max, row_sum, summed = lax.fori_loop(0, blocks, one_block, start_state)
    attended = summed / (row_sum + unseen[:, None, None])[..., None]
    return attended.reshape(text_rows, local_heads, query_count * head_dim).astype(jnp.bfloat16)


def solution(mesh):
    placed = (
        P(("segment", "seq"), "tensor"),
        P("tensor", None),
        P(),
        P("seq", "tensor", "segment"),
        P(),
        P("seq", None),
    )
    return jax.shard_map(
        shards, mesh=mesh, in_specs=placed, out_specs=P("seq", "tensor", "segment"), check_vma=False
    )
```

profile of v0, /device:TPU:1, one launch (start us, length us, event | category | flops | bytes accessed | tf_op | source)
XLA Modules:
  0.0 335.9 jit_solution(15315524799468415300)
XLA Ops:
  7.5 3.8 %fusion.30 = f32[8,96,256]{2,1,0:T(8,128)} fusion(bf16[120,8,8,256]{3,2,1,0:T(8,128)(2,1)} %bitcast.107, bf16[96,960]{1,0:T(8,128)(2,1)S(1)} %copy-done), kind=kOutput, calls=%fused_computation.41 | convolution fusion | flops 377487360 | bytes 4902912 | tf_op jit(solution)/shard_map/rd,dch->crh/dot_general | solution.py:60
  11.3 90.3 %reduce-scatter.2.cloned.1.call-done = f32[1,96,256]{2,1,0:T(8,128)} async-done(((f32[8,96,256]{2,1,0:T(8,128)}), f32[1,96,256]{2,1,0:T(8,128)}) %reduce-scatter.2.cloned.1.call-update) | async-done | bytes 98320 | tf_op jit(solution)/shard_map/reduce_scatter | solution.py:59
  105.5 124.5 %all-gather.2.cloned.1.call-done = bf16[1,6144,256]{2,1,0:T(8,128)(2,1)} async-done(((bf16[1,96,256]{2,1,0:T(8,128)(2,1)}), bf16[1,6144,256]{2,1,0:T(8,128)(2,1)}) %all-gather.2.cloned.1.call-update) | async-done | bytes 3145744 | tf_op jit(solution)/shard_map/all_gather | solution.py:84
  229.9 98.0 %while.20 = (s32[]{:T(128)}, f32[512,1,4]{0,2,1:T(4,128)S(1)}, f32[512,1,4]{0,2,1:T(4,128)S(1)}, f32[512,1,4,128]{0,3,2,1:T(8,128)S(1)}, s32[4]{0:T(128)S(1)}, /...) while((s32[]{:T(128)}, f32[512,1,4]{0,2,1:T(4,128)S(1)}, ...), condition=%wide.region_6.7_spmd.clone, body=%wide.region_2.6_spmd.clone.sunk | while | flops 828146688 | bytes 48780040 | solution.py:95
  230.5 4.8 %fusion.43 = (f32[512,4]{0,1:T(4,128)S(1)}, f32[768,512,4]{1,0,2:T(8,128)}) fusion(pred[512,768]{0,1:T(8,128)(4,1)S(1)} %compare_and_fusion.2, bf16[512,1,4,128]{3,0,2,1:T(8,128)(2,1)S(1)} %get-tuple-element.402, bf16[1,6144,256]{2,1,0:T(8,128)(2,1)} %get-tuple-element.401, s32[]{:T(128)S(6)} %select_n.147), kind=kOutput, calls=%fused_computation.2.clone.1 | convolution fusion | flops 407369728 | bytes 7413764 | tf_op jit(solution)/shard_map/while/body/eval_jaxpr/rkhd,knd->rkhn/dot_general | solution.py:32
  235.4 5.2 %fusion.46 = f32[512,1,4,128]{0,3,2,1:T(8,128)S(1)} fusion(f32[768,512,4]{1,0,2:T(8,128)} %get-tuple-element.364, f32[512,4]{0,1:T(4,128)S(1)} %bitcast.100, pred[512,768]{0,1:T(8,128)(4,1)S(1)} %compare_and_fusion.2, f32[512,1,4,128]{0,3,2,1:T(8,128)S(1)} %get-tuple-element.383, f32[512,4]{0,1:T(4,128)S(1)} %get-tuple-element.365, ...), kind=kOutput, calls=%fused_computation.10.clone.1 | convolution fusion | flops 411303936 | bytes 8994825 | tf_op jit(solution)/shard_map/while/body/eval_jaxpr/rkhn,knd->rkhd/dot_general | solution.py:47
  240.6 1.6 fusion.45
  242.8 4.8 %fusion.43 = (f32[512,4]{0,1:T(4,128)S(1)}, f32[768,512,4]{1,0,2:T(8,128)}) fusion(pred[512,768]{0,1:T(8,128)(4,1)S(1)} %compare_and_fusion.2, bf16[512,1,4,128]{3,0,2,1:T(8,128)(2,1)S(1)} %get-tuple-element.402, bf16[1,6144,256]{2,1,0:T(8,128)(2,1)} %get-tuple-element.401, s32[]{:T(128)S(6)} %select_n.147), kind=kOutput, calls=%fused_computation.2.clone.1 | convolution fusion | flops 407369728 | bytes 7413764 | tf_op jit(solution)/shard_map/while/body/eval_jaxpr/rkhd,knd->rkhn/dot_general | solution.py:32
  247.6 5.2 %fusion.46 = f32[512,1,4,128]{0,3,2,1:T(8,128)S(1)} fusion(f32[768,512,4]{1,0,2:T(8,128)} %get-tuple-element.364, f32[512,4]{0,1:T(4,128)S(1)} %bitcast.100, pred[512,768]{0,1:T(8,128)(4,1)S(1)} %compare_and_fusion.2, f32[512,1,4,128]{0,3,2,1:T(8,128)S(1)} %get-tuple-element.383, f32[512,4]{0,1:T(4,128)S(1)} %get-tuple-element.365, ...), kind=kOutput, calls=%fused_computation.10.clone.1 | convolution fusion | flops 411303936 | bytes 8994825 | tf_op jit(solution)/shard_map/while/body/eval_jaxpr/rkhn,knd->rkhd/dot_general | solution.py:47
  255.1 4.8 %fusion.43 = (f32[512,4]{0,1:T(4,128)S(1)}, f32[768,512,4]{1,0,2:T(8,128)}) fusion(pred[512,768]{0,1:T(8,128)(4,1)S(1)} %compare_and_fusion.2, bf16[512,1,4,128]{3,0,2,1:T(8,128)(2,1)S(1)} %get-tuple-element.402, bf16[1,6144,256]{2,1,0:T(8,128)(2,1)} %get-tuple-element.401, s32[]{:T(128)S(6)} %select_n.147), kind=kOutput, calls=%fused_computation.2.clone.1 | convolution fusion | flops 407369728 | bytes 7413764 | tf_op jit(solution)/shard_map/while/body/eval_jaxpr/rkhd,knd->rkhn/dot_general | solution.py:32
  259.9 5.2 %fusion.46 = f32[512,1,4,128]{0,3,2,1:T(8,128)S(1)} fusion(f32[768,512,4]{1,0,2:T(8,128)} %get-tuple-element.364, f32[512,4]{0,1:T(4,128)S(1)} %bitcast.100, pred[512,768]{0,1:T(8,128)(4,1)S(1)} %compare_and_fusion.2, f32[512,1,4,128]{0,3,2,1:T(8,128)S(1)} %get-tuple-element.383, f32[512,4]{0,1:T(4,128)S(1)} %get-tuple-element.365, ...), kind=kOutput, calls=%fused_computation.10.clone.1 | convolution fusion | flops 411303936 | bytes 8994825 | tf_op jit(solution)/shard_map/while/body/eval_jaxpr/rkhn,knd->rkhd/dot_general | solution.py:47
  265.1 1.6 fusion.45
  267.3 4.8 %fusion.43 = (f32[512,4]{0,1:T(4,128)S(1)}, f32[768,512,4]{1,0,2:T(8,128)}) fusion(pred[512,768]{0,1:T(8,128)(4,1)S(1)} %compare_and_fusion.2, bf16[512,1,4,128]{3,0,2,1:T(8,128)(2,1)S(1)} %get-tuple-element.402, bf16[1,6144,256]{2,1,0:T(8,128)(2,1)} %get-tuple-element.401, s32[]{:T(128)S(6)} %select_n.147), kind=kOutput, calls=%fused_computation.2.clone.1 | convolution fusion | flops 407369728 | bytes 7413764 | tf_op jit(solution)/shard_map/while/body/eval_jaxpr/rkhd,knd->rkhn/dot_general | solution.py:32
  272.1 5.2 %fusion.46 = f32[512,1,4,128]{0,3,2,1:T(8,128)S(1)} fusion(f32[768,512,4]{1,0,2:T(8,128)} %get-tuple-element.364, f32[512,4]{0,1:T(4,128)S(1)} %bitcast.100, pred[512,768]{0,1:T(8,128)(4,1)S(1)} %compare_and_fusion.2, f32[512,1,4,128]{0,3,2,1:T(8,128)S(1)} %get-tuple-element.383, f32[512,4]{0,1:T(4,128)S(1)} %get-tuple-element.365, ...), kind=kOutput, calls=%fused_computation.10.clone.1 | convolution fusion | flops 411303936 | bytes 8994825 | tf_op jit(solution)/shard_map/while/body/eval_jaxpr/rkhn,knd->rkhd/dot_general | solution.py:47
  279.6 4.8 %fusion.43 = (f32[512,4]{0,1:T(4,128)S(1)}, f32[768,512,4]{1,0,2:T(8,128)}) fusion(pred[512,768]{0,1:T(8,128)(4,1)S(1)} %compare_and_fusion.2, bf16[512,1,4,128]{3,0,2,1:T(8,128)(2,1)S(1)} %get-tuple-element.402, bf16[1,6144,256]{2,1,0:T(8,128)(2,1)} %get-tuple-element.401, s32[]{:T(128)S(6)} %select_n.147), kind=kOutput, calls=%fused_computation.2.clone.1 | convolution fusion | flops 407369728 | bytes 7413764 | tf_op jit(solution)/shard_map/while/body/eval_jaxpr/rkhd,knd->rkhn/dot_general | solution.py:32
  284.4 5.2 %fusion.46 = f32[512,1,4,128]{0,3,2,1:T(8,128)S(1)} fusion(f32[768,512,4]{1,0,2:T(8,128)} %get-tuple-element.364, f32[512,4]{0,1:T(4,128)S(1)} %bitcast.100, pred[512,768]{0,1:T(8,128)(4,1)S(1)} %compare_and_fusion.2, f32[512,1,4,128]{0,3,2,1:T(8,128)S(1)} %get-tuple-element.383, f32[512,4]{0,1:T(4,128)S(1)} %get-tuple-element.365, ...), kind=kOutput, calls=%fused_computation.10.clone.1 | convolution fusion | flops 411303936 | bytes 8994825 | tf_op jit(solution)/shard_map/while/body/eval_jaxpr/rkhn,knd->rkhd/dot_general | solution.py:47
  289.6 1.6 fusion.45
  291.8 4.8 %fusion.43 = (f32[512,4]{0,1:T(4,128)S(1)}, f32[768,512,4]{1,0,2:T(8,128)}) fusion(pred[512,768]{0,1:T(8,128)(4,1)S(1)} %compare_and_fusion.2, bf16[512,1,4,128]{3,0,2,1:T(8,128)(2,1)S(1)} %get-tuple-element.402, bf16[1,6144,256]{2,1,0:T(8,128)(2,1)} %get-tuple-element.401, s32[]{:T(128)S(6)} %select_n.147), kind=kOutput, calls=%fused_computation.2.clone.1 | convolution fusion | flops 407369728 | bytes 7413764 | tf_op jit(solution)/shard_map/while/body/eval_jaxpr/rkhd,knd->rkhn/dot_general | solution.py:32
  296.6 5.2 %fusion.46 = f32[512,1,4,128]{0,3,2,1:T(8,128)S(1)} fusion(f32[768,512,4]{1,0,2:T(8,128)} %get-tuple-element.364, f32[512,4]{0,1:T(4,128)S(1)} %bitcast.100, pred[512,768]{0,1:T(8,128)(4,1)S(1)} %compare_and_fusion.2, f32[512,1,4,128]{0,3,2,1:T(8,128)S(1)} %get-tuple-element.383, f32[512,4]{0,1:T(4,128)S(1)} %get-tuple-element.365, ...), kind=kOutput, calls=%fused_computation.10.clone.1 | convolution fusion | flops 411303936 | bytes 8994825 | tf_op jit(solution)/shard_map/while/body/eval_jaxpr/rkhn,knd->rkhd/dot_general | solution.py:47
  304.1 4.8 %fusion.43 = (f32[512,4]{0,1:T(4,128)S(1)}, f32[768,512,4]{1,0,2:T(8,128)}) fusion(pred[512,768]{0,1:T(8,128)(4,1)S(1)} %compare_and_fusion.2, bf16[512,1,4,128]{3,0,2,1:T(8,128)(2,1)S(1)} %get-tuple-element.402, bf16[1,6144,256]{2,1,0:T(8,128)(2,1)} %get-tuple-element.401, s32[]{:T(128)S(6)} %select_n.147), kind=kOutput, calls=%fused_computation.2.clone.1 | convolution fusion | flops 407369728 | bytes 7413764 | tf_op jit(solution)/shard_map/while/body/eval_jaxpr/rkhd,knd->rkhn/dot_general | solution.py:32
  308.9 5.2 %fusion.46 = f32[512,1,4,128]{0,3,2,1:T(8,128)S(1)} fusion(f32[768,512,4]{1,0,2:T(8,128)} %get-tuple-element.364, f32[512,4]{0,1:T(4,128)S(1)} %bitcast.100, pred[512,768]{0,1:T(8,128)(4,1)S(1)} %compare_and_fusion.2, f32[512,1,4,128]{0,3,2,1:T(8,128)S(1)} %get-tuple-element.383, f32[512,4]{0,1:T(4,128)S(1)} %get-tuple-element.365, ...), kind=kOutput, calls=%fused_computation.10.clone.1 | convolution fusion | flops 411303936 | bytes 8994825 | tf_op jit(solution)/shard_map/while/body/eval_jaxpr/rkhn,knd->rkhd/dot_general | solution.py:47
  314.1 1.6 fusion.45
  316.3 4.8 %fusion.43 = (f32[512,4]{0,1:T(4,128)S(1)}, f32[768,512,4]{1,0,2:T(8,128)}) fusion(pred[512,768]{0,1:T(8,128)(4,1)S(1)} %compare_and_fusion.2, bf16[512,1,4,128]{3,0,2,1:T(8,128)(2,1)S(1)} %get-tuple-element.402, bf16[1,6144,256]{2,1,0:T(8,128)(2,1)} %get-tuple-element.401, s32[]{:T(128)S(6)} %select_n.147), kind=kOutput, calls=%fused_computation.2.clone.1 | convolution fusion | flops 407369728 | bytes 7413764 | tf_op jit(solution)/shard_map/while/body/eval_jaxpr/rkhd,knd->rkhn/dot_general | solution.py:32
  321.1 5.2 %fusion.46 = f32[512,1,4,128]{0,3,2,1:T(8,128)S(1)} fusion(f32[768,512,4]{1,0,2:T(8,128)} %get-tuple-element.364, f32[512,4]{0,1:T(4,128)S(1)} %bitcast.100, pred[512,768]{0,1:T(8,128)(4,1)S(1)} %compare_and_fusion.2, f32[512,1,4,128]{0,3,2,1:T(8,128)S(1)} %get-tuple-element.383, f32[512,4]{0,1:T(4,128)S(1)} %get-tuple-element.365, ...), kind=kOutput, calls=%fused_computation.10.clone.1 | convolution fusion | flops 411303936 | bytes 8994825 | tf_op jit(solution)/shard_map/while/body/eval_jaxpr/rkhn,knd->rkhd/dot_general | solution.py:47
  (103 shorter events, 17.2 us)
Async XLA Ops:
  6.5 0.9 copy-start
  6.5 98.4 %copy-start.2 = (bf16[512,1,512]{2,0,1:T(8,128)(2,1)S(1)}, bf16[512,1,512]{2,0,1:T(8,128)(2,1)}, u32[]{:S(2)}) copy-start(bf16[512,1,512]{2,0,1:T(8,128)(2,1)} %param.11) | copy-start | bytes 1572868
  6.5 98.9 %copy-start.3 = (s32[512,2]{0,1:T(2,128)S(1)}, s32[512,2]{0,1:T(2,128)}, u32[]{:S(2)}) copy-start(s32[512,2]{0,1:T(2,128)} %param.13) | copy-start | bytes 12292
  6.5 223.4 %copy-start.4 = (s32[4]{0:T(128)S(1)}, s32[4]{0:T(128)}, u32[]{:S(2)}) copy-start(s32[4]{0:T(128)} %param.12) | copy-start | bytes 52
  6.5 95.0 %reduce-scatter.2.cloned.1.call-start = ((), (), s32[]{:S(2)}) async-start(), calls=%async_computation.1 | async-start | bytes 884736 | tf_op jit(solution)/shard_map/reduce_scatter | solution.py:59
  11.2 218.7 %all-gather.2.cloned.1.call-start = ((), (), s32[]{:S(2)}) async-start(), calls=%async_computation.2 | async-start | bytes 3194880 | tf_op jit(solution)/shard_map/all_gather | solution.py:84
  235.4 5.2 %copy-start.1 = (f32[768,512,4]{1,0,2:T(8,128)S(1)}, f32[768,512,4]{1,0,2:T(8,128)}, u32[]{:S(2)}) copy-start(f32[768,512,4]{1,0,2:T(8,128)} %get-tuple-element.364) | copy-start | bytes 18874372 | tf_op jit(solution)/shard_map/while
  247.6 5.2 %copy-start.1 = (f32[768,512,4]{1,0,2:T(8,128)S(1)}, f32[768,512,4]{1,0,2:T(8,128)}, u32[]{:S(2)}) copy-start(f32[768,512,4]{1,0,2:T(8,128)} %get-tuple-element.364) | copy-start | bytes 18874372 | tf_op jit(solution)/shard_map/while
  259.9 5.2 %copy-start.1 = (f32[768,512,4]{1,0,2:T(8,128)S(1)}, f32[768,512,4]{1,0,2:T(8,128)}, u32[]{:S(2)}) copy-start(f32[768,512,4]{1,0,2:T(8,128)} %get-tuple-element.364) | copy-start | bytes 18874372 | tf_op jit(solution)/shard_map/while
  272.1 5.2 %copy-start.1 = (f32[768,512,4]{1,0,2:T(8,128)S(1)}, f32[768,512,4]{1,0,2:T(8,128)}, u32[]{:S(2)}) copy-start(f32[768,512,4]{1,0,2:T(8,128)} %get-tuple-element.364) | copy-start | bytes 18874372 | tf_op jit(solution)/shard_map/while
  284.4 5.2 %copy-start.1 = (f32[768,512,4]{1,0,2:T(8,128)S(1)}, f32[768,512,4]{1,0,2:T(8,128)}, u32[]{:S(2)}) copy-start(f32[768,512,4]{1,0,2:T(8,128)} %get-tuple-element.364) | copy-start | bytes 18874372 | tf_op jit(solution)/shard_map/while
  296.6 5.2 %copy-start.1 = (f32[768,512,4]{1,0,2:T(8,128)S(1)}, f32[768,512,4]{1,0,2:T(8,128)}, u32[]{:S(2)}) copy-start(f32[768,512,4]{1,0,2:T(8,128)} %get-tuple-element.364) | copy-start | bytes 18874372 | tf_op jit(solution)/shard_map/while
  308.9 5.2 %copy-start.1 = (f32[768,512,4]{1,0,2:T(8,128)S(1)}, f32[768,512,4]{1,0,2:T(8,128)}, u32[]{:S(2)}) copy-start(f32[768,512,4]{1,0,2:T(8,128)} %get-tuple-element.364) | copy-start | bytes 18874372 | tf_op jit(solution)/shard_map/while
  321.1 5.2 %copy-start.1 = (f32[768,512,4]{1,0,2:T(8,128)S(1)}, f32[768,512,4]{1,0,2:T(8,128)}, u32[]{:S(2)}) copy-start(f32[768,512,4]{1,0,2:T(8,128)} %get-tuple-element.364) | copy-start | bytes 18874372 | tf_op jit(solution)/shard_map/while
Sparse Core Ops, SparseCore 0:
  11.8 89.7 reduce-scatter.1
  105.0 124.9 all-gather.1
where the time goes:
time: 336 us
  waiting for transfers between devices  215 us (64%)
  matrix products  83.5 us (25%)
  other arithmetic  20.1 us (6%)
  between operations  13.5 us (4%)
    all_gather x1, waiting for transfers between devices, shards(): gathered = lax.all_gather(kv_block, ('segment', 'seq'), axis=1, tiled=True)  124 us
    reduce_scatter x1, waiting for transfers between devices, shards(): lax.psum_scatter(jnp.einsum('rd,dch->crh', vision_states, weight_heads, p...  90.3 us
    dot_general x8, matrix products, update(): jnp.einsum('rkhn,knd->rkhd', weights, kv_piece[:, :, head_dim:], preferre...  41.4 us
    dot_general x8, matrix products, update(): jnp.einsum('rkhd,knd->rkhn', query_heads, kv_piece[:, :, :head_dim], pref...  38.4 us
    reduce_sum x8, other arithmetic, update(): row_sum = row_sum * factor + jnp.sum(expterm, axis=-1)  12.6 us
  transfers between devices with their start and end apart: 2, of which 2 were waited for; matrix products, arithmetic and copies ran while one was open for 0% of the time, Pallas kernels for 0%

commit v1 on v0

--- a/solution.py
+++ b/solution.py
@@ -81,7 +81,12 @@
         jnp.zeros((text_rows, local_heads, query_count), jnp.float32),
         jnp.zeros((text_rows, local_heads, query_count, head_dim), jnp.float32),
     )
-    gathered = lax.all_gather(kv_block, ("segment", "seq"), axis=1, tiled=True)
+    gathered = jnp.concatenate(
+        lax.all_to_all(
+            jnp.stack([kv_block] * lax.axis_size(("segment", "seq"))), ("segment", "seq"), 0, 0
+        ),
+        axis=1,
+    )
     total_rows = gathered.shape[1]
     blocks = block_count(total_rows, 768)
     block_rows = total_rows // blocks

time: 336 us -> 370 us (1.10)
  waiting for transfers between devices: 215 us -> 231 us
  starting transfers between devices: 0.08 us -> 15.6 us
    all_to_all x0 -> x1, waiting for transfers between devices: none -> 140 us  [shards(): lax.all_to_all(jnp.stack([kv_block] * lax.axis_size(('segment', 'seq'))),...]
    all_gather x1 -> x0, waiting for transfers between devices: 124 us -> none  [shards(): gathered = lax.all_gather(kv_block, ('segment', 'seq'), axis=1, tiled=True)]
    all_to_all x0 -> x1, starting transfers between devices: none -> 15.6 us  [shards(): lax.all_to_all(jnp.stack([kv_block] * lax.axis_size(('segment', 'seq'))),...]
where the time goes in v1:
time: 370 us; the launch traced here: 369 us
  waiting for transfers between devices  231 us (62%)
  matrix products  83.6 us (23%)
  other arithmetic  19.5 us (5%)
  starting transfers between devices  15.6 us (4%)
  between operations  13.5 us (4%)
  local copies, waits for them, and re-layouts  5.39 us (1%)
    all_to_all x1, waiting for transfers between devices, shards(): lax.all_to_all(jnp.stack([kv_block] * lax.axis_size(('segment', 'seq'))),...  140 us
    reduce_scatter x1, waiting for transfers between devices, shards(): lax.psum_scatter(jnp.einsum('rd,dch->crh', vision_states, weight_heads, p...  90.7 us
    dot_general x8, matrix products, update(): jnp.einsum('rkhn,knd->rkhd', weights, kv_piece[:, :, head_dim:], preferre...  41.4 us
    dot_general x8, matrix products, update(): jnp.einsum('rkhd,knd->rkhn', query_heads, kv_piece[:, :, :head_dim], pref...  38.4 us
    all_to_all x1, starting transfers between devices, shards(): lax.all_to_all(jnp.stack([kv_block] * lax.axis_size(('segment', 'seq'))),...  15.6 us
    reduce_sum x8, other arithmetic, update(): row_sum = row_sum * factor + jnp.sum(expterm, axis=-1)  12.6 us
  transfers between devices with their start and end apart: 2, of which 2 were waited for; matrix products, arithmetic and copies ran while one was open for 0% of the time, Pallas kernels for 0%

profile of v1, /device:TPU:1, one launch (start us, length us, event | category | flops | bytes accessed | tf_op | source)
XLA Modules:
  0.0 369.4 jit_solution(16309100796999602713)
XLA Ops:
  7.5 3.8 %fusion.30 = f32[8,96,256]{2,1,0:T(8,128)} fusion(bf16[120,8,8,256]{3,2,1,0:T(8,128)(2,1)} %bitcast.112, bf16[96,960]{1,0:T(8,128)(2,1)S(1)} %copy-done), kind=kOutput, calls=%fused_computation.41 | convolution fusion | flops 377487360 | bytes 4902912 | tf_op jit(solution)/shard_map/rd,dch->crh/dot_general | solution.py:60
  11.2 90.7 %reduce-scatter.2.cloned.1.call-done = f32[1,96,256]{2,1,0:T(8,128)} async-done(((f32[8,96,256]{2,1,0:T(8,128)}), f32[1,96,256]{2,1,0:T(8,128)}) %reduce-scatter.2.cloned.1.call-update) | async-done | bytes 98320 | tf_op jit(solution)/shard_map/reduce_scatter | solution.py:59
  104.6 2.0 stack.2
  106.6 15.6 %all-to-all-start = ((bf16[64,1,96,256]{3,2,1,0:T(8,128)(2,1)}), bf16[64,1,96,256]{3,2,1,0:T(8,128)(2,1)}, u32[]{:S(2)}, u32[]{:S(2)}) async-start(bf16[64,1,96,256]{3,2,1,0:T(8,128)(2,1)} %stack.2), calls=%async_computation.1 | async-start | bytes 6291456 | tf_op jit(solution)/shard_map/all_to_all | solution.py:85
  122.9 140.4 %all-to-all-done = bf16[64,1,96,256]{3,2,1,0:T(8,128)(2,1)} async-done(((bf16[64,1,96,256]{3,2,1,0:T(8,128)(2,1)}), bf16[64,1,96,256]{3,2,1,0:T(8,128)(2,1)}, u32[]{:S(2)}, u32[]{:S(2)}) %all-to-all-start) | async-done | bytes 3145760 | tf_op jit(solution)/shard_map/all_to_all | solution.py:85
  263.3 98.1 %while.20 = (s32[]{:T(128)}, f32[512,1,4]{0,2,1:T(4,128)S(1)}, f32[512,1,4]{0,2,1:T(4,128)S(1)}, f32[512,1,4,128]{0,3,2,1:T(8,128)S(1)}, s32[4]{0:T(128)S(1)}, /...) while((s32[]{:T(128)}, f32[512,1,4]{0,2,1:T(4,128)S(1)}, ...), condition=%wide.region_6.7_spmd.clone, body=%wide.region_2.6_spmd.clone.sunk | while | flops 828146688 | bytes 48780040 | solution.py:100
  263.9 4.8 %fusion.45 = (f32[512,4]{0,1:T(4,128)S(1)}, f32[768,512,4]{1,0,2:T(8,128)}) fusion(pred[512,768]{0,1:T(8,128)(4,1)S(1)} %compare_and_fusion.2, bf16[512,1,4,128]{3,0,2,1:T(8,128)(2,1)S(1)} %get-tuple-element.411, bf16[1,6144,256]{2,1,0:T(8,128)(2,1)} %get-tuple-element.410, s32[]{:T(128)S(6)} %select_n.147), kind=kOutput, calls=%fused_computation.2.clone.1 | convolution fusion | flops 407369728 | bytes 7413764 | tf_op jit(solution)/shard_map/while/body/eval_jaxpr/rkhd,knd->rkhn/dot_general | solution.py:32
  268.7 5.2 %fusion.48 = f32[512,1,4,128]{0,3,2,1:T(8,128)S(1)} fusion(f32[768,512,4]{1,0,2:T(8,128)} %get-tuple-element.373, f32[512,4]{0,1:T(4,128)S(1)} %bitcast.105, pred[512,768]{0,1:T(8,128)(4,1)S(1)} %compare_and_fusion.2, f32[512,1,4,128]{0,3,2,1:T(8,128)S(1)} %get-tuple-element.392, f32[512,4]{0,1:T(4,128)S(1)} %get-tuple-element.374, ...), kind=kOutput, calls=%fused_computation.10.clone.1 | convolution fusion | flops 411303936 | bytes 8994825 | tf_op jit(solution)/shard_map/while/body/eval_jaxpr/rkhn,knd->rkhd/dot_general | solution.py:47
  276.2 4.8 %fusion.45 = (f32[512,4]{0,1:T(4,128)S(1)}, f32[768,512,4]{1,0,2:T(8,128)}) fusion(pred[512,768]{0,1:T(8,128)(4,1)S(1)} %compare_and_fusion.2, bf16[512,1,4,128]{3,0,2,1:T(8,128)(2,1)S(1)} %get-tuple-element.411, bf16[1,6144,256]{2,1,0:T(8,128)(2,1)} %get-tuple-element.410, s32[]{:T(128)S(6)} %select_n.147), kind=kOutput, calls=%fused_computation.2.clone.1 | convolution fusion | flops 407369728 | bytes 7413764 | tf_op jit(solution)/shard_map/while/body/eval_jaxpr/rkhd,knd->rkhn/dot_general | solution.py:32
  281.0 5.2 %fusion.48 = f32[512,1,4,128]{0,3,2,1:T(8,128)S(1)} fusion(f32[768,512,4]{1,0,2:T(8,128)} %get-tuple-element.373, f32[512,4]{0,1:T(4,128)S(1)} %bitcast.105, pred[512,768]{0,1:T(8,128)(4,1)S(1)} %compare_and_fusion.2, f32[512,1,4,128]{0,3,2,1:T(8,128)S(1)} %get-tuple-element.392, f32[512,4]{0,1:T(4,128)S(1)} %get-tuple-element.374, ...), kind=kOutput, calls=%fused_computation.10.clone.1 | convolution fusion | flops 411303936 | bytes 8994825 | tf_op jit(solution)/shard_map/while/body/eval_jaxpr/rkhn,knd->rkhd/dot_general | solution.py:47
  286.2 1.6 fusion.47
  288.4 4.8 %fusion.45 = (f32[512,4]{0,1:T(4,128)S(1)}, f32[768,512,4]{1,0,2:T(8,128)}) fusion(pred[512,768]{0,1:T(8,128)(4,1)S(1)} %compare_and_fusion.2, bf16[512,1,4,128]{3,0,2,1:T(8,128)(2,1)S(1)} %get-tuple-element.411, bf16[1,6144,256]{2,1,0:T(8,128)(2,1)} %get-tuple-element.410, s32[]{:T(128)S(6)} %select_n.147), kind=kOutput, calls=%fused_computation.2.clone.1 | convolution fusion | flops 407369728 | bytes 7413764 | tf_op jit(solution)/shard_map/while/body/eval_jaxpr/rkhd,knd->rkhn/dot_general | solution.py:32
  293.3 5.2 %fusion.48 = f32[512,1,4,128]{0,3,2,1:T(8,128)S(1)} fusion(f32[768,512,4]{1,0,2:T(8,128)} %get-tuple-element.373, f32[512,4]{0,1:T(4,128)S(1)} %bitcast.105, pred[512,768]{0,1:T(8,128)(4,1)S(1)} %compare_and_fusion.2, f32[512,1,4,128]{0,3,2,1:T(8,128)S(1)} %get-tuple-element.392, f32[512,4]{0,1:T(4,128)S(1)} %get-tuple-element.374, ...), kind=kOutput, calls=%fused_computation.10.clone.1 | convolution fusion | flops 411303936 | bytes 8994825 | tf_op jit(solution)/shard_map/while/body/eval_jaxpr/rkhn,knd->rkhd/dot_general | solution.py:47
  300.7 4.8 %fusion.45 = (f32[512,4]{0,1:T(4,128)S(1)}, f32[768,512,4]{1,0,2:T(8,128)}) fusion(pred[512,768]{0,1:T(8,128)(4,1)S(1)} %compare_and_fusion.2, bf16[512,1,4,128]{3,0,2,1:T(8,128)(2,1)S(1)} %get-tuple-element.411, bf16[1,6144,256]{2,1,0:T(8,128)(2,1)} %get-tuple-element.410, s32[]{:T(128)S(6)} %select_n.147), kind=kOutput, calls=%fused_computation.2.clone.1 | convolution fusion | flops 407369728 | bytes 7413764 | tf_op jit(solution)/shard_map/while/body/eval_jaxpr/rkhd,knd->rkhn/dot_general | solution.py:32
  305.5 5.2 %fusion.48 = f32[512,1,4,128]{0,3,2,1:T(8,128)S(1)} fusion(f32[768,512,4]{1,0,2:T(8,128)} %get-tuple-element.373, f32[512,4]{0,1:T(4,128)S(1)} %bitcast.105, pred[512,768]{0,1:T(8,128)(4,1)S(1)} %compare_and_fusion.2, f32[512,1,4,128]{0,3,2,1:T(8,128)S(1)} %get-tuple-element.392, f32[512,4]{0,1:T(4,128)S(1)} %get-tuple-element.374, ...), kind=kOutput, calls=%fused_computation.10.clone.1 | convolution fusion | flops 411303936 | bytes 8994825 | tf_op jit(solution)/shard_map/while/body/eval_jaxpr/rkhn,knd->rkhd/dot_general | solution.py:47
  313.0 4.8 %fusion.45 = (f32[512,4]{0,1:T(4,128)S(1)}, f32[768,512,4]{1,0,2:T(8,128)}) fusion(pred[512,768]{0,1:T(8,128)(4,1)S(1)} %compare_and_fusion.2, bf16[512,1,4,128]{3,0,2,1:T(8,128)(2,1)S(1)} %get-tuple-element.411, bf16[1,6144,256]{2,1,0:T(8,128)(2,1)} %get-tuple-element.410, s32[]{:T(128)S(6)} %select_n.147), kind=kOutput, calls=%fused_computation.2.clone.1 | convolution fusion | flops 407369728 | bytes 7413764 | tf_op jit(solution)/shard_map/while/body/eval_jaxpr/rkhd,knd->rkhn/dot_general | solution.py:32
  317.8 5.2 %fusion.48 = f32[512,1,4,128]{0,3,2,1:T(8,128)S(1)} fusion(f32[768,512,4]{1,0,2:T(8,128)} %get-tuple-element.373, f32[512,4]{0,1:T(4,128)S(1)} %bitcast.105, pred[512,768]{0,1:T(8,128)(4,1)S(1)} %compare_and_fusion.2, f32[512,1,4,128]{0,3,2,1:T(8,128)S(1)} %get-tuple-element.392, f32[512,4]{0,1:T(4,128)S(1)} %get-tuple-element.374, ...), kind=kOutput, calls=%fused_computation.10.clone.1 | convolution fusion | flops 411303936 | bytes 8994825 | tf_op jit(solution)/shard_map/while/body/eval_jaxpr/rkhn,knd->rkhd/dot_general | solution.py:47
  323.0 1.6 fusion.47
  325.2 4.8 %fusion.45 = (f32[512,4]{0,1:T(4,128)S(1)}, f32[768,512,4]{1,0,2:T(8,128)}) fusion(pred[512,768]{0,1:T(8,128)(4,1)S(1)} %compare_and_fusion.2, bf16[512,1,4,128]{3,0,2,1:T(8,128)(2,1)S(1)} %get-tuple-element.411, bf16[1,6144,256]{2,1,0:T(8,128)(2,1)} %get-tuple-element.410, s32[]{:T(128)S(6)} %select_n.147), kind=kOutput, calls=%fused_computation.2.clone.1 | convolution fusion | flops 407369728 | bytes 7413764 | tf_op jit(solution)/shard_map/while/body/eval_jaxpr/rkhd,knd->rkhn/dot_general | solution.py:32
  330.1 5.2 %fusion.48 = f32[512,1,4,128]{0,3,2,1:T(8,128)S(1)} fusion(f32[768,512,4]{1,0,2:T(8,128)} %get-tuple-element.373, f32[512,4]{0,1:T(4,128)S(1)} %bitcast.105, pred[512,768]{0,1:T(8,128)(4,1)S(1)} %compare_and_fusion.2, f32[512,1,4,128]{0,3,2,1:T(8,128)S(1)} %get-tuple-element.392, f32[512,4]{0,1:T(4,128)S(1)} %get-tuple-element.374, ...), kind=kOutput, calls=%fused_computation.10.clone.1 | convolution fusion | flops 411303936 | bytes 8994825 | tf_op jit(solution)/shard_map/while/body/eval_jaxpr/rkhn,knd->rkhd/dot_general | solution.py:47
  337.5 4.8 %fusion.45 = (f32[512,4]{0,1:T(4,128)S(1)}, f32[768,512,4]{1,0,2:T(8,128)}) fusion(pred[512,768]{0,1:T(8,128)(4,1)S(1)} %compare_and_fusion.2, bf16[512,1,4,128]{3,0,2,1:T(8,128)(2,1)S(1)} %get-tuple-element.411, bf16[1,6144,256]{2,1,0:T(8,128)(2,1)} %get-tuple-element.410, s32[]{:T(128)S(6)} %select_n.147), kind=kOutput, calls=%fused_computation.2.clone.1 | convolution fusion | flops 407369728 | bytes 7413764 | tf_op jit(solution)/shard_map/while/body/eval_jaxpr/rkhd,knd->rkhn/dot_general | solution.py:32
  342.3 5.2 %fusion.48 = f32[512,1,4,128]{0,3,2,1:T(8,128)S(1)} fusion(f32[768,512,4]{1,0,2:T(8,128)} %get-tuple-element.373, f32[512,4]{0,1:T(4,128)S(1)} %bitcast.105, pred[512,768]{0,1:T(8,128)(4,1)S(1)} %compare_and_fusion.2, f32[512,1,4,128]{0,3,2,1:T(8,128)S(1)} %get-tuple-element.392, f32[512,4]{0,1:T(4,128)S(1)} %get-tuple-element.374, ...), kind=kOutput, calls=%fused_computation.10.clone.1 | convolution fusion | flops 411303936 | bytes 8994825 | tf_op jit(solution)/shard_map/while/body/eval_jaxpr/rkhn,knd->rkhd/dot_general | solution.py:47
  349.7 4.8 %fusion.45 = (f32[512,4]{0,1:T(4,128)S(1)}, f32[768,512,4]{1,0,2:T(8,128)}) fusion(pred[512,768]{0,1:T(8,128)(4,1)S(1)} %compare_and_fusion.2, bf16[512,1,4,128]{3,0,2,1:T(8,128)(2,1)S(1)} %get-tuple-element.411, bf16[1,6144,256]{2,1,0:T(8,128)(2,1)} %get-tuple-element.410, s32[]{:T(128)S(6)} %select_n.147), kind=kOutput, calls=%fused_computation.2.clone.1 | convolution fusion | flops 407369728 | bytes 7413764 | tf_op jit(solution)/shard_map/while/body/eval_jaxpr/rkhd,knd->rkhn/dot_general | solution.py:32
  354.6 5.2 %fusion.48 = f32[512,1,4,128]{0,3,2,1:T(8,128)S(1)} fusion(f32[768,512,4]{1,0,2:T(8,128)} %get-tuple-element.373, f32[512,4]{0,1:T(4,128)S(1)} %bitcast.105, pred[512,768]{0,1:T(8,128)(4,1)S(1)} %compare_and_fusion.2, f32[512,1,4,128]{0,3,2,1:T(8,128)S(1)} %get-tuple-element.392, f32[512,4]{0,1:T(4,128)S(1)} %get-tuple-element.374, ...), kind=kOutput, calls=%fused_computation.10.clone.1 | convolution fusion | flops 411303936 | bytes 8994825 | tf_op jit(solution)/shard_map/while/body/eval_jaxpr/rkhn,knd->rkhd/dot_general | solution.py:47
  (103 shorter events, 19.7 us)
Async XLA Ops:
  6.5 0.9 copy-start
  6.5 95.4 %reduce-scatter.2.cloned.1.call-start = ((), (), s32[]{:S(2)}) async-start(), calls=%async_computation.2 | async-start | bytes 884736 | tf_op jit(solution)/shard_map/reduce_scatter | solution.py:59
  11.2 111.1 %copy-start.2 = (bf16[512,1,512]{2,0,1:T(8,128)(2,1)S(1)}, bf16[512,1,512]{2,0,1:T(8,128)(2,1)}, u32[]{:S(2)}) copy-start(bf16[512,1,512]{2,0,1:T(8,128)(2,1)} %param.11) | copy-start | bytes 1572868
  11.2 111.7 %copy-start.3 = (s32[512,2]{0,1:T(2,128)S(1)}, s32[512,2]{0,1:T(2,128)}, u32[]{:S(2)}) copy-start(s32[512,2]{0,1:T(2,128)} %param.13) | copy-start | bytes 12292
  11.2 252.1 %copy-start.4 = (s32[4]{0:T(128)S(1)}, s32[4]{0:T(128)}, u32[]{:S(2)}) copy-start(s32[4]{0:T(128)} %param.12) | copy-start | bytes 52
  106.6 156.7 %all-to-all-start = ((bf16[64,1,96,256]{3,2,1,0:T(8,128)(2,1)}), bf16[64,1,96,256]{3,2,1,0:T(8,128)(2,1)}, u32[]{:S(2)}, u32[]{:S(2)}) async-start(bf16[64,1,96,256]{3,2,1,0:T(8,128)(2,1)} %stack.2), calls=%async_computation.1 | async-start | bytes 6291456 | tf_op jit(solution)/shard_map/all_to_all | solution.py:85
  268.7 5.2 %copy-start.1 = (f32[768,512,4]{1,0,2:T(8,128)S(1)}, f32[768,512,4]{1,0,2:T(8,128)}, u32[]{:S(2)}) copy-start(f32[768,512,4]{1,0,2:T(8,128)} %get-tuple-element.373) | copy-start | bytes 18874372 | tf_op jit(solution)/shard_map/while
  281.0 5.2 %copy-start.1 = (f32[768,512,4]{1,0,2:T(8,128)S(1)}, f32[768,512,4]{1,0,2:T(8,128)}, u32[]{:S(2)}) copy-start(f32[768,512,4]{1,0,2:T(8,128)} %get-tuple-element.373) | copy-start | bytes 18874372 | tf_op jit(solution)/shard_map/while
  293.3 5.2 %copy-start.1 = (f32[768,512,4]{1,0,2:T(8,128)S(1)}, f32[768,512,4]{1,0,2:T(8,128)}, u32[]{:S(2)}) copy-start(f32[768,512,4]{1,0,2:T(8,128)} %get-tuple-element.373) | copy-start | bytes 18874372 | tf_op jit(solution)/shard_map/while
  305.5 5.2 %copy-start.1 = (f32[768,512,4]{1,0,2:T(8,128)S(1)}, f32[768,512,4]{1,0,2:T(8,128)}, u32[]{:S(2)}) copy-start(f32[768,512,4]{1,0,2:T(8,128)} %get-tuple-element.373) | copy-start | bytes 18874372 | tf_op jit(solution)/shard_map/while
  317.8 5.2 %copy-start.1 = (f32[768,512,4]{1,0,2:T(8,128)S(1)}, f32[768,512,4]{1,0,2:T(8,128)}, u32[]{:S(2)}) copy-start(f32[768,512,4]{1,0,2:T(8,128)} %get-tuple-element.373) | copy-start | bytes 18874372 | tf_op jit(solution)/shard_map/while
  330.0 5.2 %copy-start.1 = (f32[768,512,4]{1,0,2:T(8,128)S(1)}, f32[768,512,4]{1,0,2:T(8,128)}, u32[]{:S(2)}) copy-start(f32[768,512,4]{1,0,2:T(8,128)} %get-tuple-element.373) | copy-start | bytes 18874372 | tf_op jit(solution)/shard_map/while
  342.3 5.2 %copy-start.1 = (f32[768,512,4]{1,0,2:T(8,128)S(1)}, f32[768,512,4]{1,0,2:T(8,128)}, u32[]{:S(2)}) copy-start(f32[768,512,4]{1,0,2:T(8,128)} %get-tuple-element.373) | copy-start | bytes 18874372 | tf_op jit(solution)/shard_map/while
  354.6 5.2 %copy-start.1 = (f32[768,512,4]{1,0,2:T(8,128)S(1)}, f32[768,512,4]{1,0,2:T(8,128)}, u32[]{:S(2)}) copy-start(f32[768,512,4]{1,0,2:T(8,128)} %get-tuple-element.373) | copy-start | bytes 18874372 | tf_op jit(solution)/shard_map/while
Sparse Core Ops, SparseCore 0:
  11.8 90.1 reduce-scatter.1
